TPU v7x, 128 devices: a whole 4x4x4 slice. The times are simulated.
128 devices in a mesh: row: 8 (over y, z_lo), col: 16 (over x, z_hi, core).
Axes of the slice: x: 4, y: 4, z: 4 (z_hi: 2, z_lo: 2; z = z_hi * 2 + z_lo), core: 2. Of those that a mesh axis runs over, the one named last changes fastest.
Arguments:
- tokens: bfloat16 [1024, 53248], P(('row', 'col')), may hold values from -6 to 6
- eigvecs: float32 [53248, 2048], P('row', 'col'), may hold values from -0.02734375 to 0.02734375
- eigvals: float32 [2048], P('col'), may hold values from 0.25 to 4
- v_first: float32 [53248, 256], P(('row', 'col')), may hold values from -0.109375 to 0.109375
- v_second: float32 [53248, 256], P(('row', 'col')), may hold values from -0.109375 to 0.109375
- t_first: float32 [256, 256], replicated, may hold values from -0.375 to 0.375
- t_second: float32 [256, 256], replicated, may hold values from -0.375 to 0.375
Outputs:
- whitened: float32 [1024, 2048], P('row', 'col')
All inputs are finite; a program needn't handle non-finite values.
Results may differ from a plain program's by a relative error of at most 0.0029.
Values may be sent and summed in bfloat16 or wider, within the bound.
A program may use at most 128 MiB of HBM per device.

v0:
```python
import jax
import jax.numpy as jnp
from jax import lax
from jax.sharding import PartitionSpec as P


def local_update(block, panel, factor, inner):
    middle = jnp.dot(
        factor, inner, precision=lax.Precision.HIGHEST, preferred_element_type=jnp.float32
    )
    return block - jnp.dot(
        panel, middle, precision=lax.Precision.HIGHEST, preferred_element_type=jnp.float32
    )


def partial_inner(panel, block):
    return jnp.dot(
        panel.T, block, precision=lax.Precision.HIGHEST, preferred_element_type=jnp.float32
    )


def per_device(tokens, eigvecs, eigvals, v_first, v_second, t_first, t_second):
    panels = (
        lax.all_gather(v_first, "col", axis=0, tiled=True),
        lax.all_gather(v_second, "col", axis=0, tiled=True),
    )
    block = eigvecs
    for panel, factor in ((panels[1], t_second), (panels[0], t_first)):
        inner = lax.psum(partial_inner(panel, block), "row")
        block = local_update(block, panel, factor, inner)
    whitening = (block * lax.rsqrt(eigvals)[None, :]).astype(jnp.bfloat16)
    row_tokens = lax.all_gather(tokens, "col", axis=0, tiled=True)
    slab = lax.all_to_all(row_tokens, "row", split_axis=1, concat_axis=0, tiled=True)
    partial_value = jnp.dot(slab, whitening, preferred_element_type=jnp.float32)
    summed = lax.psum_scatter(partial_value, "row", scatter_dimension=0, tiled=True)
    return summed


def solution(mesh):
    in_specs = (
        P(("row", "col"), None),
        P("row", "col"),
        P("col"),
        P(("row", "col"), None),
        P(("row", "col"), None),
        P(),
        P(),
    )
    out_specs = P("row", "col")
    return jax.shard_map(
        per_device, mesh=mesh, in_specs=in_specs, out_specs=out_specs, check_vma=False
    )
```

profile of v0, /device:TPU:0, one launch (start us, length us, event | category | flops | bytes accessed | tf_op | source)
XLA Modules:
  0.0 653.4 jit_solution(17153606568712980208)
XLA Ops:
  6.5 0.7 all-gather.4.cloned.1.call-update
  7.3 0.0 all-gather.8.cloned.1.call-start
  7.3 0.7 all-gather.8.cloned.1.call-update
  8.0 0.0 all-reduce.3.cloned.1.call-start
  8.1 70.6 %all-gather.4.cloned.1.call-done = f32[6656,256]{1,0:T(8,128)} async-done(((f32[416,256]{1,0:T(8,128)}), f32[6656,256]{1,0:T(8,128)}) %all-gather.4.cloned.1.call-update) | async-done | bytes 6815760 | tf_op jit(solution)/shard_map/all_gather | solution.py:25
  78.7 14.6 %fusion.4 = f32[256,128]{1,0:T(8,128)} fusion(f32[6656,256]{1,0:T(8,128)} %all-gather.4.cloned.1.call-done, f32[6656,128]{1,0:T(8,128)} %param.8), kind=kOutput, calls=%fused_computation.8 | convolution fusion | flops 2617245696 | bytes 10354688 | tf_op jit(solution)/shard_map/dot_general | solution.py:17
  93.3 0.0 all-reduce.3.cloned.1.call-update
  93.4 0.0 all-gather.6.cloned.1.call-start
  93.4 0.5 all-gather.6.cloned.1.call-update
  94.0 80.9 %all-gather.8.cloned.1.call-done = bf16[128,53248]{1,0:T(8,128)(2,1)} async-done(((bf16[8,53248]{1,0:T(8,128)(2,1)}), bf16[128,53248]{1,0:T(8,128)(2,1)}) %all-gather.8.cloned.1.call-update) | async-done | bytes 13631504 | tf_op jit(solution)/shard_map/all_gather | solution.py:32
  174.8 18.4 %copy.17 = bf16[128,53248]{0,1:T(8,128)(2,1)} copy(bf16[128,53248]{1,0:T(8,128)(2,1)} %all-gather.8.cloned.1.call-done) | data formatting | bytes 27262976 | tf_op jit(solution)/shard_map/all_gather | solution.py:32
  193.2 5.4 all-to-all-start
  198.7 0.2 all-reduce.5.cloned.1.call-start
  198.9 5.1 copy.16
  204.0 216.3 %all-reduce.3.cloned.1.call-done = f32[256,128]{1,0:T(8,128)} async-done(((f32[256,128]{1,0:T(8,128)}), f32[256,128]{1,0:T(8,128)}) %all-reduce.3.cloned.1.call-update) | async-done | bytes 131088 | tf_op jit(solution)/shard_map/psum | solution.py:29
  420.3 0.0 copy-done
  420.3 1.3 fusion.5
  421.6 12.6 %fusion.2 = f32[6656,128]{0,1:T(8,128)} fusion(f32[6656,128]{0,1:T(8,128)} %copy.16, f32[128,256]{1,0:T(8,128)S(1)} %fusion.5, f32[6656,256]{1,0:T(8,128)} %all-gather.4.cloned.1.call-done), kind=kOutput, calls=%fused_computation.4 | convolution fusion | flops 2618097664 | bytes 13762560 | tf_op jit(solution)/shard_map/dot_general | solution.py:11
  434.2 54.4 %all-gather.6.cloned.1.call-done = f32[6656,256]{1,0:T(8,128)} async-done(((f32[416,256]{1,0:T(8,128)}), f32[6656,256]{1,0:T(8,128)}) %all-gather.6.cloned.1.call-update) | async-done | bytes 6815760 | tf_op jit(solution)/shard_map/all_gather | solution.py:24
  488.6 7.9 %convolution_bitcast_fusion.3 = f32[256,128]{0,1:T(8,128)} fusion(f32[6656,128]{0,1:T(8,128)} %fusion.2, f32[6656,256]{1,0:T(8,128)} %all-gather.6.cloned.1.call-done), kind=kOutput, calls=%fused_computation.7 | convolution fusion | flops 2617245696 | bytes 10354688 | tf_op jit(solution)/shard_map/dot_general | solution.py:17
  496.5 0.0 all-reduce.5.cloned.1.call-update
  496.5 0.3 reduce-scatter.2.cloned.1.call-start
  496.8 0.0 copy-done.3
  496.8 71.0 %all-reduce.5.cloned.1.call-done = f32[256,128]{0,1:T(8,128)} async-done(((f32[256,128]{0,1:T(8,128)}), f32[256,128]{0,1:T(8,128)}) %all-reduce.5.cloned.1.call-update) | async-done | bytes 131088 | tf_op jit(solution)/shard_map/psum | solution.py:29
  567.8 1.3 fusion.6
  569.1 10.8 %fusion.3 = bf16[6656,128]{0,1:T(8,128)(2,1)S(1)} fusion(f32[6656,128]{0,1:T(8,128)} %fusion.2, f32[128,256]{1,0:T(8,128)S(1)} %fusion.6, f32[6656,256]{1,0:T(8,128)} %all-gather.6.cloned.1.call-done, f32[128]{0:T(128)S(1)} %rsqrt.3), kind=kOutput, calls=%fused_computation.5 | convolution fusion | flops 2619801600 | bytes 12059136 | tf_op jit(solution)/shard_map/dot_general | solution.py:11
  579.9 0.0 all-to-all-done
  579.9 17.6 %copy.18 = bf16[8,128,6656]{2,1,0:T(8,128)(2,1)} copy(bf16[8,128,6656]{1,2,0:T(8,128)(2,1)} %bitcast.4) | data formatting | bytes 27262976 | tf_op jit(solution)/shard_map/all_to_all | solution.py:33
  597.5 10.1 %convolution_bitcast_fusion.2 = f32[1024,128]{0,1:T(8,128)} fusion(bf16[6656,128]{0,1:T(8,128)(2,1)S(1)} %fusion.3, bf16[1024,6656]{1,0:T(8,128)(2,1)} %bitcast.34), kind=kOutput, calls=%fused_computation.6 | convolution fusion | flops 1744830464 | bytes 15859712 | tf_op jit(solution)/shard_map/dot_general | solution.py:34
  607.6 0.0 reduce-scatter.2.cloned.1.call-update
  607.6 37.4 %reduce-scatter.2.cloned.1.call-done = f32[128,128]{0,1:T(8,128)} async-done(((f32[1024,128]{0,1:T(8,128)}), f32[128,128]{0,1:T(8,128)}) %reduce-scatter.2.cloned.1.call-update) | async-done | bytes 65552 | tf_op jit(solution)/shard_map/reduce_scatter | solution.py:35
  645.0 1.6 copy.19
  (8 shorter events, 0.0 us)
Async XLA Ops:
  6.5 413.8 %copy-start = (f32[256,256]{1,0:T(8,128)S(1)}, f32[256,256]{1,0:T(8,128)}, u32[]{:S(2)}) copy-start(f32[256,256]{1,0:T(8,128)} %param.13) | copy-start | bytes 786436
  6.5 72.2 %all-gather.4.cloned.1.call-start = ((), (), s32[]{:S(2)}) async-start(), calls=%async_computation.2 | async-start | bytes 7241728 | tf_op jit(solution)/shard_map/all_gather | solution.py:25
  7.3 167.6 %all-gather.8.cloned.1.call-start = ((), (), s32[]{:S(2)}) async-start(), calls=%async_computation.6 | async-start | bytes 14483456 | tf_op jit(solution)/shard_map/all_gather | solution.py:32
  8.0 412.3 %all-reduce.3.cloned.1.call-start = ((), (), s32[]{:S(2)}) async-start(), calls=%async_computation.3 | async-start | bytes 262144 | tf_op jit(solution)/shard_map/psum | solution.py:29
  93.4 395.2 %all-gather.6.cloned.1.call-start = ((), (), s32[]{:S(2)}) async-start(), calls=%async_computation.4 | async-start | bytes 7241728 | tf_op jit(solution)/shard_map/all_gather | solution.py:24
  193.2 386.7 %all-to-all-start = ((bf16[128,8,6656]{0,2,1:T(8,128)(2,1)}), bf16[128,8,6656]{0,2,1:T(8,128)(2,1)}, u32[]{:S(2)}, u32[]{:S(2)}) async-start(bf16[128,8,6656]{0,2,1:T(8,128)(2,1)} %bitcast.33), calls=%async_computation | async-start | bytes 27262976 | tf_op jit(solution)/shard_map/all_to_all | solution.py:33
  198.7 369.1 %all-reduce.5.cloned.1.call-start = ((), (), s32[]{:S(2)}) async-start(), calls=%async_computation.5 | async-start | bytes 262144 | tf_op jit(solution)/shard_map/psum | solution.py:29
  434.2 62.6 %copy-start.3 = (f32[128]{0:T(128)S(1)}, f32[128]{0:T(128)}, u32[]{:S(2)}) copy-start(f32[128]{0:T(128)} %param.9) | copy-start | bytes 1540
  434.2 133.6 %copy-start.2 = (f32[256,256]{1,0:T(8,128)S(1)}, f32[256,256]{1,0:T(8,128)}, u32[]{:S(2)}) copy-start(f32[256,256]{1,0:T(8,128)} %param.12) | copy-start | bytes 786436
  496.5 148.5 %reduce-scatter.2.cloned.1.call-start = ((), (), s32[]{:S(2)}) async-start(), calls=%async_computation.7 | async-start | bytes 589824 | tf_op jit(solution)/shard_map/reduce_scatter | solution.py:35
  597.5 49.1 %copy-start.1 = (f32[256,256]{1,0:T(8,128)S(1)}, f32[256,256]{1,0:T(8,128)}, u32[]{:S(2)}) copy-start(f32[256,256]{1,0:T(8,128)} %param.13) | copy-start | bytes 786436
Sparse Core Ops, SparseCore 0:
  9.8 68.8 all-gather.3
  81.1 93.6 all-gather.7
  177.3 242.9 all-reduce.2
  422.8 65.6 all-gather.5
  496.6 71.0 all-reduce.4
  607.7 37.2 reduce-scatter.1
where the time goes:
time: 655 us; the launch traced here: 653 us
  waiting for transfers between devices  533 us (81%)
  matrix products  58.7 us (9%)
  local copies, waits for them, and re-layouts  42.6 us (7%)
  between operations  13.5 us (2%)
    psum x2, waiting for transfers between devices, per_device(): inner = lax.psum(partial_inner(panel, block), 'row')  287 us
    all_gather x1, waiting for transfers between devices, per_device(): row_tokens = lax.all_gather(tokens, 'col', axis=0, tiled=True)  80.9 us
    all_gather x1, waiting for transfers between devices, per_device(): lax.all_gather(v_second, 'col', axis=0, tiled=True)  70.6 us
    all_gather x1, waiting for transfers between devices, per_device(): lax.all_gather(v_first, 'col', axis=0, tiled=True)  54.4 us
    reduce_scatter x1, waiting for transfers between devices, per_device(): lax.psum_scatter(partial_value, 'row', scatter_dimension=0, tiled=True)  37.4 us
    dot_general x2, matrix products, local_update(): jnp.dot(panel, middle, precision=lax.Precision.HIGHEST, preferred_element...  23.4 us
    dot_general x2, matrix products, partial_inner(): jnp.dot(panel.T, block, precision=lax.Precision.HIGHEST, preferred_elemen...  22.6 us
    all_gather x1, local copies, waits for them, and re-layouts, per_device(): row_tokens = lax.all_gather(tokens, 'col', axis=0, tiled=True)  18.4 us
  transfers between devices with their start and end apart: 7, of which 6 were waited for; matrix products, arithmetic and copies ran while one was open for 11% of the time, Pallas kernels for 0%

commit v1 on v0

--- a/solution.py
+++ b/solution.py
@@ -26,7 +26,7 @@
     )
     block = eigvecs
     for panel, factor in ((panels[1], t_second), (panels[0], t_first)):
-        inner = lax.psum(partial_inner(panel, block), "row")
+        inner = jnp.sum(lax.all_gather(partial_inner(panel, block), "row"), axis=0)
         block = local_update(block, panel, factor, inner)
     whitening = (block * lax.rsqrt(eigvals)[None, :]).astype(jnp.bfloat16)
     row_tokens = lax.all_gather(tokens, "col", axis=0, tiled=True)

time: 655 us -> 589 us (0.90)
  waiting for transfers between devices: 533 us -> 465 us
    psum x2 -> x0, waiting for transfers between devices: 287 us -> none  [per_device(): inner = lax.psum(partial_inner(panel, block), 'row')]
    all_gather x0 -> x2, waiting for transfers between devices: none -> 188 us  [per_device(): inner = jnp.sum(lax.all_gather(partial_inner(panel, block), 'row'), axis=0)]
    all_gather x1, waiting for transfers between devices: 54.4 us -> 85.4 us  [per_device(): lax.all_gather(v_first, 'col', axis=0, tiled=True)]
  transfers between devices with their start and end apart: 7 -> 7, of which waited for: 6 -> 6; matrix products, arithmetic and copies ran while one was open for 11% -> 12% of each run, Pallas kernels for 0% -> 0%
where the time goes in v1:
time: 589 us; the launch traced here: 587 us
  waiting for transfers between devices  465 us (79%)
  matrix products  56.9 us (10%)
  local copies, waits for them, and re-layouts  44.2 us (8%)
  between operations  13.6 us (2%)
  starting transfers between devices  6.05 us (1%)
    all_gather x2, waiting for transfers between devices, per_device(): inner = jnp.sum(lax.all_gather(partial_inner(panel, block), 'row'), axis=0)  188 us
    all_gather x1, waiting for transfers between devices, per_device(): lax.all_gather(v_first, 'col', axis=0, tiled=True)  85.4 us
    all_gather x1, waiting for transfers between devices, per_device(): row_tokens = lax.all_gather(tokens, 'col', axis=0, tiled=True)  80.9 us
    all_gather x1, waiting for transfers between devices, per_device(): lax.all_gather(v_second, 'col', axis=0, tiled=True)  70.6 us
    reduce_scatter x1, waiting for transfers between devices, per_device(): lax.psum_scatter(partial_value, 'row', scatter_dimension=0, tiled=True)  37.8 us
    dot_general x2, matrix products, local_update(): jnp.dot(panel, middle, precision=lax.Precision.HIGHEST, preferred_element...  23.4 us
    dot_general x2, matrix products, partial_inner(): jnp.dot(panel.T, block, precision=lax.Precision.HIGHEST, preferred_elemen...  22.5 us
    all_gather x1, local copies, waits for them, and re-layouts, per_device(): row_tokens = lax.all_gather(tokens, 'col', axis=0, tiled=True)  18.4 us
  transfers between devices with their start and end apart: 7, of which 6 were waited for; matrix products, arithmetic and copies ran while one was open for 12% of the time, Pallas kernels for 0%

profile of v1, /device:TPU:0, one launch (start us, length us, event | category | flops | bytes accessed | tf_op | source)
XLA Modules:
  0.0 587.3 jit_solution(6696955592179137621)
XLA Ops:
  6.5 0.7 all-gather.8.cloned.1.call-update
  7.3 0.0 all-gather.12.cloned.1.call-start
  7.3 0.7 all-gather.12.cloned.1.call-update
  8.0 0.0 all-gather.14.cloned.1.call-start
  8.1 70.6 %all-gather.8.cloned.1.call-done = f32[6656,256]{1,0:T(8,128)} async-done(((f32[416,256]{1,0:T(8,128)}), f32[6656,256]{1,0:T(8,128)}) %all-gather.8.cloned.1.call-update) | async-done | bytes 6815760 | tf_op jit(solution)/shard_map/all_gather | solution.py:25
  78.7 14.6 %fusion.4 = f32[256,128]{1,0:T(8,128)} fusion(f32[6656,256]{1,0:T(8,128)} %all-gather.8.cloned.1.call-done, f32[6656,128]{1,0:T(8,128)} %param.8), kind=kOutput, calls=%fused_computation.9 | convolution fusion | flops 2617245696 | bytes 10354688 | tf_op jit(solution)/shard_map/dot_general | solution.py:17
  93.3 0.0 all-gather.14.cloned.1.call-update
  93.3 0.0 all-gather.10.cloned.1.call-start
  93.4 0.5 all-gather.10.cloned.1.call-update
  93.9 80.9 %all-gather.12.cloned.1.call-done = bf16[128,53248]{1,0:T(8,128)(2,1)} async-done(((bf16[8,53248]{1,0:T(8,128)(2,1)}), bf16[128,53248]{1,0:T(8,128)(2,1)}) %all-gather.12.cloned.1.call-update) | async-done | bytes 13631504 | tf_op jit(solution)/shard_map/all_gather | solution.py:32
  174.8 18.4 %copy.17 = bf16[128,53248]{0,1:T(8,128)(2,1)} copy(bf16[128,53248]{1,0:T(8,128)(2,1)} %all-gather.12.cloned.1.call-done) | data formatting | bytes 27262976 | tf_op jit(solution)/shard_map/all_gather | solution.py:32
  193.2 5.4 all-to-all-start
  198.7 0.2 all-gather.16.cloned.1.call-start
  198.9 5.1 copy.16
  204.0 151.5 %all-gather.14.cloned.1.call-done = f32[2048,128]{1,0:T(8,128)} async-done(((f32[256,128]{1,0:T(8,128)}), f32[2048,128]{1,0:T(8,128)}) %all-gather.14.cloned.1.call-update) | async-done | bytes 1048592 | tf_op jit(solution)/shard_map/all_gather | solution.py:29
  355.5 1.3 reduce_sum.18
  356.8 0.4 fusion.5
  357.2 12.6 %fusion.2 = f32[6656,128]{0,1:T(8,128)} fusion(f32[6656,128]{0,1:T(8,128)} %copy.16, f32[128,256]{1,0:T(8,128)S(1)} %fusion.5, f32[6656,256]{1,0:T(8,128)} %all-gather.8.cloned.1.call-done), kind=kOutput, calls=%fused_computation.4 | convolution fusion | flops 2618097664 | bytes 13762560 | tf_op jit(solution)/shard_map/dot_general | solution.py:11
  369.8 85.4 %all-gather.10.cloned.1.call-done = f32[6656,256]{1,0:T(8,128)} async-done(((f32[416,256]{1,0:T(8,128)}), f32[6656,256]{1,0:T(8,128)}) %all-gather.10.cloned.1.call-update) | async-done | bytes 6815760 | tf_op jit(solution)/shard_map/all_gather | solution.py:24
  455.2 7.9 %convolution_bitcast_fusion.3 = f32[256,128]{0,1:T(8,128)} fusion(f32[6656,128]{0,1:T(8,128)} %fusion.2, f32[6656,256]{1,0:T(8,128)} %all-gather.10.cloned.1.call-done), kind=kOutput, calls=%fused_computation.7 | convolution fusion | flops 2617245696 | bytes 10354688 | tf_op jit(solution)/shard_map/dot_general | solution.py:17
  463.1 0.0 all-gather.16.cloned.1.call-update
  463.1 0.3 reduce-scatter.2.cloned.1.call-start
  463.4 36.8 %all-gather.16.cloned.1.call-done = f32[2048,128]{0,1:T(8,128)} async-done(((f32[256,128]{0,1:T(8,128)}), f32[2048,128]{0,1:T(8,128)}) %all-gather.16.cloned.1.call-update) | async-done | bytes 1048592 | tf_op jit(solution)/shard_map/all_gather | solution.py:29
  500.2 1.6 copy.20
  501.8 0.3 bitcast_reduce_fusion
  502.1 0.4 fusion.6
  502.5 10.8 %fusion.3 = bf16[6656,128]{0,1:T(8,128)(2,1)S(1)} fusion(f32[6656,128]{0,1:T(8,128)} %fusion.2, f32[128,256]{1,0:T(8,128)S(1)} %fusion.6, f32[6656,256]{1,0:T(8,128)} %all-gather.10.cloned.1.call-done, f32[128]{0:T(128)S(1)} %rsqrt.3), kind=kOutput, calls=%fused_computation.5 | convolution fusion | flops 2619801600 | bytes 12059136 | tf_op jit(solution)/shard_map/dot_general | solution.py:11
  513.3 17.6 %copy.18 = bf16[8,128,6656]{2,1,0:T(8,128)(2,1)} copy(bf16[8,128,6656]{1,2,0:T(8,128)(2,1)} %bitcast.5) | data formatting | bytes 27262976 | tf_op jit(solution)/shard_map/all_to_all | solution.py:33
  530.9 10.1 %convolution_bitcast_fusion.2 = f32[1024,128]{0,1:T(8,128)} fusion(bf16[6656,128]{0,1:T(8,128)(2,1)S(1)} %fusion.3, bf16[1024,6656]{1,0:T(8,128)(2,1)} %bitcast.40), kind=kOutput, calls=%fused_computation.6 | convolution fusion | flops 1744830464 | bytes 15859712 | tf_op jit(solution)/shard_map/dot_general | solution.py:34
  541.0 0.0 reduce-scatter.2.cloned.1.call-update
  541.0 37.8 %reduce-scatter.2.cloned.1.call-done = f32[128,128]{0,1:T(8,128)} async-done(((f32[1024,128]{0,1:T(8,128)}), f32[128,128]{0,1:T(8,128)}) %reduce-scatter.2.cloned.1.call-update) | async-done | bytes 65552 | tf_op jit(solution)/shard_map/reduce_scatter | solution.py:35
  578.9 1.6 copy.19
  (11 shorter events, 0.0 us)
Async XLA Ops:
  6.5 350.3 %copy-start = (f32[256,256]{1,0:T(8,128)S(1)}, f32[256,256]{1,0:T(8,128)}, u32[]{:S(2)}) copy-start(f32[256,256]{1,0:T(8,128)} %param.13) | copy-start | bytes 786436
  6.5 72.2 %all-gather.8.cloned.1.call-start = ((), (), s32[]{:S(2)}) async-start(), calls=%async_computation.2 | async-start | bytes 7241728 | tf_op jit(solution)/shard_map/all_gather | solution.py:25
  7.3 167.6 %all-gather.12.cloned.1.call-start = ((), (), s32[]{:S(2)}) async-start(), calls=%async_computation.4 | async-start | bytes 14483456 | tf_op jit(solution)/shard_map/all_gather | solution.py:32
  8.0 347.5 %all-gather.14.cloned.1.call-start = ((), (), s32[]{:S(2)}) async-start(), calls=%async_computation.6 | async-start | bytes 1179648 | tf_op jit(solution)/shard_map/all_gather | solution.py:29
  93.3 361.8 %all-gather.10.cloned.1.call-start = ((), (), s32[]{:S(2)}) async-start(), calls=%async_computation.3 | async-start | bytes 7241728 | tf_op jit(solution)/shard_map/all_gather | solution.py:24
  193.2 320.1 %all-to-all-start = ((bf16[128,8,6656]{0,2,1:T(8,128)(2,1)}), bf16[128,8,6656]{0,2,1:T(8,128)(2,1)}, u32[]{:S(2)}, u32[]{:S(2)}) async-start(bf16[128,8,6656]{0,2,1:T(8,128)(2,1)} %bitcast.39), calls=%async_computation | async-start | bytes 27262976 | tf_op jit(solution)/shard_map/all_to_all | solution.py:33
  198.7 301.6 %all-gather.16.cloned.1.call-start = ((), (), s32[]{:S(2)}) async-start(), calls=%async_computation.7 | async-start | bytes 1179648 | tf_op jit(solution)/shard_map/all_gather | solution.py:29
  369.8 93.6 %copy-start.3 = (f32[128]{0:T(128)S(1)}, f32[128]{0:T(128)}, u32[]{:S(2)}) copy-start(f32[128]{0:T(128)} %param.9) | copy-start | bytes 1540
  463.1 39.0 %copy-start.2 = (f32[256,256]{1,0:T(8,128)S(1)}, f32[256,256]{1,0:T(8,128)}, u32[]{:S(2)}) copy-start(f32[256,256]{1,0:T(8,128)} %param.12) | copy-start | bytes 786436
  463.1 115.7 %reduce-scatter.2.cloned.1.call-start = ((), (), s32[]{:S(2)}) async-start(), calls=%async_computation.5 | async-start | bytes 589824 | tf_op jit(solution)/shard_map/reduce_scatter | solution.py:35
  530.9 49.5 %copy-start.1 = (f32[256,256]{1,0:T(8,128)S(1)}, f32[256,256]{1,0:T(8,128)}, u32[]{:S(2)}) copy-start(f32[256,256]{1,0:T(8,128)} %param.13) | copy-start | bytes 786436
Sparse Core Ops, SparseCore 0:
  9.8 68.8 all-gather.7
  81.1 93.6 all-gather.11
  176.5 179.0 all-gather.13
  357.8 97.3 all-gather.9
  463.3 36.9 all-gather.15
  541.2 37.6 reduce-scatter.1
